TPU v7x, 512 devices: a whole 4x4x16 slice. The times are simulated.
512 devices in a mesh: seq: 16 (over x, y_hi, core), head: 32 (over z, y_lo).
Axes of the slice: x: 4, y: 4 (y_hi: 2, y_lo: 2; y = y_hi * 2 + y_lo), z: 16, core: 2. Of those that a mesh axis runs over, the one named last changes fastest.
Arguments:
- x_inner: bfloat16 [24576, 16384], P('seq', 'head'), may hold values from -400 to 400
- z_gate: bfloat16 [24576, 16384], P('seq', 'head'), may hold values from -6 to 6
- bc_raw: bfloat16 [24576, 512], P(('seq', 'head')), may hold values from -6 to 6
- conv_weight: float32 [4, 512], replicated, may hold values from -3 to 3
- conv_bias: float32 [512], replicated, may hold values from -3 to 3
- dt_raw: float32 [24576, 128], P('seq', 'head'), may hold values from -6 to 24576
- a_log: float32 [128], P('head'), may hold values from -20 to 1
- d_skip: float32 [128], P('head'), may hold values from 0.5 to 1.5
- norm_gain: float32 [16384], P('head'), may hold values from 0.5 to 1.5
Outputs:
- mixer_out: bfloat16 [24576, 16384], P('seq', 'head')
All inputs are finite; a program needn't handle non-finite values.
Results may differ from a plain program's by a relative error of at most 0.0034.
Values may be sent and summed in bfloat16 or wider, within the bound.
A program may use at most 64 MiB of HBM per device.

v0:
```python
import jax
import jax.numpy as jnp
from jax import lax
from jax.sharding import PartitionSpec as P

HEAD_DIM = 128
STATE = 256
BLOCK = 256
INNER = 16384


def shifted(shard, axis, by):
    length = lax.axis_size(axis)
    pairs = [(i, i + by) for i in range(length) if 0 <= i + by < length]
    return lax.ppermute(shard, axis, pairs)


def prefix(part, axis, combine, identity):
    place = lax.axis_index(axis)
    gathered = jax.tree.map(lambda a: lax.all_gather(a, axis), part)
    state = jax.tree.map(lambda a, e: jnp.zeros_like(a) + jnp.asarray(e, a.dtype), part, identity)

    def one(hop, state):
        return combine(
            state, jax.tree.map(lambda a: lax.dynamic_index_in_dim(a, hop, 0, False), gathered)
        )

    return lax.fori_loop(0, place, one, state)


def convolve_rows(padded, conv_weight, conv_bias):
    tap_count = conv_weight.shape[0]
    row_count = padded.shape[0] - tap_count + 1
    padded_float = padded.astype(jnp.float32)
    accumulated = jnp.broadcast_to(conv_bias[None, :], (row_count, padded.shape[1]))
    for offset in range(tap_count):
        accumulated = (
            accumulated + conv_weight[offset][None, :] * padded_float[offset : offset + row_count]
        )
    return jax.nn.silu(accumulated).astype(jnp.bfloat16)


def on_device(x_inner, z_gate, bc_raw, conv_weight, conv_bias, dt_raw, a_log, d_skip, norm_gain):
    highest = lax.Precision.HIGHEST
    rim_count = conv_weight.shape[0] - 1
    gathered = lax.all_gather(bc_raw, "head", axis=0, tiled=True)
    rim_rows = shifted(gathered[-rim_count:], "seq", 1)
    bc_act = convolve_rows(jnp.concatenate([rim_rows, gathered], axis=0), conv_weight, conv_bias)
    length = x_inner.shape[0]
    head_count = a_log.shape[0]
    block_count = length // BLOCK
    step_size = jax.nn.softplus(dt_raw)
    log_step = -jnp.exp(a_log)[None, :] * step_size
    cum_log = jnp.cumsum(log_step.reshape(block_count, BLOCK, head_count), axis=1)
    size_blocks = step_size.reshape(block_count, BLOCK, head_count)
    b_blocks = bc_act[:, :STATE].reshape(block_count, BLOCK, STATE)
    c_blocks = bc_act[:, STATE:].reshape(block_count, BLOCK, STATE)
    x_float = x_inner.astype(jnp.float32).reshape(block_count, BLOCK, head_count, HEAD_DIM)
    gram_blocks = jnp.einsum("cin,cjn->cij", c_blocks, b_blocks, preferred_element_type=jnp.float32)
    lower_mask = jnp.tril(jnp.ones((BLOCK, BLOCK), dtype=bool))
    by_head = jnp.transpose(cum_log, (0, 2, 1))
    spread = by_head[:, :, :, None] - by_head[:, :, None, :]
    decay_blocks = jnp.where(lower_mask, jnp.exp(jnp.where(lower_mask, spread, 0.0)), 0.0)
    weights = (
        gram_blocks[:, None] * decay_blocks * jnp.transpose(size_blocks, (0, 2, 1))[:, :, None, :]
    )
    inner_part = jnp.einsum("chij,cjhp->cihp", weights, x_float, precision=highest)
    tail_weight = jnp.exp(cum_log[:, -1:, :] - cum_log) * size_blocks
    block_states = jnp.einsum(
        "cjhp,cjn->chpn",
        x_float * tail_weight[..., None],
        b_blocks.astype(jnp.float32),
        precision=highest,
    )
    block_decay = jnp.exp(cum_log[:, -1, :])
    zero_state = jnp.zeros((head_count, HEAD_DIM, STATE), jnp.float32)
    starts = []
    current = zero_state
    for block_index in range(block_count):
        starts.append(current)
        current = block_decay[block_index][:, None, None] * current + block_states[block_index]
    zero_starts = jnp.stack(starts)
    log_total = jnp.sum(cum_log[:, -1, :], axis=0)

    def combine(earlier, later):
        return (earlier[0] + later[0], jnp.exp(later[0])[:, None, None] * earlier[1] + later[1])

    identity = (jnp.zeros_like(log_total), zero_state)
    chained = prefix((log_total, current), "seq", combine, identity)
    incoming = chained[1]
    c_float = c_blocks.astype(jnp.float32)
    carried_part = jnp.exp(cum_log)[..., None] * jnp.einsum(
        "cin,chpn->cihp", c_float, zero_starts, precision=highest
    )
    prior_log = jnp.cumsum(cum_log[:, -1, :], axis=0) - cum_log[:, -1, :]
    entry_part = jnp.exp(cum_log + prior_log[:, None, :])[..., None] * jnp.einsum(
        "cin,hpn->cihp", c_float, incoming, precision=highest
    )
    carried_part = carried_part + entry_part
    ssm_out = inner_part + carried_part + d_skip[None, None, :, None] * x_float
    gated_out = ssm_out.reshape(length, head_count * HEAD_DIM) * jax.nn.silu(
        z_gate.astype(jnp.float32)
    )
    square_sum = lax.psum(jnp.sum(gated_out * gated_out, axis=1), "head")
    inverse_rms = lax.rsqrt(square_sum / INNER + 1e-05)
    return (gated_out * inverse_rms[:, None] * norm_gain[None, :]).astype(jnp.bfloat16)


def solution(mesh):
    placed = (
        P("seq", "head"),
        P("seq", "head"),
        P(("seq", "head"), None),
        P(),
        P(),
        P("seq", "head"),
        P("head"),
        P("head"),
        P("head"),
    )
    return jax.shard_map(
        on_device, mesh=mesh, in_specs=placed, out_specs=P("seq", "head"), check_vma=False
    )
```

profile of v0, /device:TPU:22, one launch (start us, length us, event | category | flops | bytes accessed | tf_op | source)
XLA Modules:
  0.0 351.3 jit_solution(10148498477770559478)
XLA Ops:
  6.5 0.7 all-gather.4.cloned.1.call-update
  7.3 0.7 exponential_negate_fusion
  8.0 0.8 broadcast_multiply_fusion
  8.8 7.2 %reduce-window.6 = f32[6,4,2,128]{3,2,1,0:T(2,128)S(1)} reduce-window(f32[6,4,2,128]{3,2,1,0:T(2,128)S(1)} %copy.59, f32[]{:T(128)} %constant.42.clone.1), window={size=1x1x1x128 pad=0_0x0_0x0_0x127_0}, to_apply=%region_0.1 | reduce-window | flops 780288 | bytes 49156 | tf_op jit(solution)/shard_map/reduce-window
  16.7 0.2 subtract_reduce_fusion
  16.9 0.8 broadcast_dynamic-update-slice_fusion
  17.7 0.9 fusion.36
  18.7 127.5 %all-gather.4.cloned.1.call-done = bf16[1536,512]{1,0:T(8,128)(2,1)} async-done(((bf16[48,512]{1,0:T(8,128)(2,1)}), bf16[1536,512]{1,0:T(8,128)(2,1)}) %all-gather.4.cloned.1.call-update) | async-done | bytes 1572880 | tf_op jit(solution)/shard_map/all_gather | solution.py:46
  146.2 0.8 slice.108
  147.1 1.9 collective-permute-start
  149.0 0.3 slice_reduce_fusion.1
  149.2 2.4 reshape.86
  151.6 1.8 collective-permute-done
  153.5 0.5 maximum_convert_fusion
  154.0 2.0 multiply_convert_fusion.1
  156.1 4.3 %fusion.7 = f32[6,4,128,256]{3,2,1,0:T(8,128)S(1)} fusion(bf16[6,256,256,1]{2,1,3,0:T(8,128)(2,1)S(1)} %bitcast.69, f32[6,256,4]{1,2,0:T(4,128)S(1)} %copy.52, bf16[6,256,4,128]{3,2,1,0:T(4,128)(2,1)S(1)} %reshape.86), kind=kOutput, calls=%fused_computation.13 | convolution fusion | flops 2417491968 | bytes 5529600 | tf_op jit(solution)/shard_map/cjhp,cjn->chpn/dot_general | solution.py:69
  160.5 0.1 constant_dynamic-update-slice_fusion.1
  160.8 0.2 constant_dynamic-update-slice_fusion
  161.0 1.0 fusion.30
  162.0 1.8 copy-done.2
  163.8 1.3 dynamic-slice
  165.7 0.2 dynamic-update-slice
  165.9 27.4 %all-reduce = f32[64]{0:T(128)S(1)} all-reduce(f32[64]{0:T(128)S(1)} %dynamic-update-slice), channel_id=2, replica_groups=mesh['seq'=16,'head'=32] {'seq'}, use_global_device_ids=true, to_apply=%add | all-reduce | flops 64 | bytes 512
  193.5 0.4 fusion.37
  193.9 6.0 %fusion = f32[6,4,256,128]{3,2,1,0:T(8,128)} fusion(f32[6,4,256]{2,1,0:T(4,128)S(1)} %copy.47, f32[6,4,256]{2,1,0:T(4,128)S(1)} %reduce_window_sum.35, f32[6,256,256]{2,1,0:T(8,128)S(1)} %fusion.37, pred[256,256]{1,0:T(8,128)(4,1)S(1)} %iota_compare_fusion, bf16[6,256,4,128]{3,2,1,0:T(4,128)(2,1)S(1)} %reshape.86), kind=kOutput, calls=%fused_computation.2 | convolution fusion | flops 2423783424 | bytes 6406144 | tf_op jit(solution)/shard_map/chij,cjhp->cihp/dot_general | solution.py:67
  199.9 46.5 %all-gather.6.cloned.1.call-done = f32[16,4,128,256]{3,2,1,0:T(8,128)} async-done(((f32[1,4,128,256]{3,2,1,0:T(8,128)}), f32[16,4,128,256]{3,2,1,0:T(8,128)}) %all-gather.6.cloned.1.call-update) | async-done | bytes 8388624 | tf_op jit(solution)/shard_map/all_gather | solution.py:20
  246.4 17.7 %while.12 = (s32[]{:T(128)}, f32[4,128,256]{2,1,0:T(8,128)S(1)}, s32[]{:T(128)}, f32[16,4]{1,0:T(8,128)S(1)}, f32[16,4,128,256]{3,2,1,0:T(8,128)}, /*index=5*/s32[]{:T(128)}, s32[]{:T(128)}, s32[]{:T(128)}) while((s32[]{:T(128)}, f32[4,128,256]{2,1,0:T(8,128)S(1)}, s32[]{:T(128)}, f32[16,4]{1,0:T(8,128)S(1)}, f32[16,4,128,256]{3,2,1,0:T(8,128)}, ...), condition=%wide.region_5.6_spmd, body=%wide.region_4.5_spmd.sunk | while | flops 262149 | bytes 1573039 | solution.py:28
  246.5 1.2 bitcast_add_fusion.3
  247.7 1.2 bitcast_add_fusion.3
  249.0 1.2 bitcast_add_fusion.3
  250.2 1.2 bitcast_add_fusion.3
  251.5 1.2 bitcast_add_fusion.3
  252.7 1.2 bitcast_add_fusion.3
  254.0 1.2 bitcast_add_fusion.3
  255.2 1.2 bitcast_add_fusion.3
  256.5 1.2 bitcast_add_fusion.3
  257.7 1.2 bitcast_add_fusion.3
  259.0 1.2 bitcast_add_fusion.3
  260.2 1.2 bitcast_add_fusion.3
  261.5 1.2 bitcast_add_fusion.3
  262.7 1.2 bitcast_add_fusion.3
  264.1 1.5 fusion.26
  265.6 0.4 copy-done.3
  266.0 5.3 %fusion.8 = f32[6,256,4,128]{3,1,2,0:T(8,128)S(1)} fusion(f32[6,4,256,128]{3,2,1,0:T(8,128)} %fusion, f32[6,256,4,128]{3,1,2,0:T(8,128)S(1)} %fusion.26, bf16[6,256,256,1]{2,1,3,0:T(8,128)(2,1)S(1)} %bitcast.68, f32[6,4,128,256]{3,2,1,0:T(8,128)S(1)} %copy-done.3, f32[4]{0:T(128)S(1)} %copy-done.7, f32[6,256,4]{1,2,0:T(4,128)S(1)} %copy.54, ...), kind=kOutput, calls=%fused_computation.14 | convolution fusion | flops 2421424128 | bytes 14991376 | tf_op jit(solution)/shard_map/cin,chpn->cihp/dot_general | solution.py:92
  271.3 2.0 copy.55
  273.4 1.0 multiply_reduce_fusion
  274.4 66.5 %psum.7 = f32[1536]{0:T(1024)S(1)} all-reduce(f32[1536]{0:T(1024)S(1)} %multiply_reduce_fusion), channel_id=1, replica_groups=mesh['seq'=16,'head'=32] {'head'}, use_global_device_ids=true, to_apply=%region_7.8 | all-reduce | flops 1536 | bytes 12288 | tf_op jit(solution)/shard_map/psum | solution.py:104
  341.0 3.5 multiply_convert_fusion
  (59 shorter events, 1.6 us)
Async XLA Ops:
  6.5 139.7 %all-gather.4.cloned.1.call-start = ((), (), s32[]{:S(2)}) async-start(), calls=%async_computation | async-start | bytes 1622016 | tf_op jit(solution)/shard_map/all_gather | solution.py:46
  7.3 239.1 %all-gather.6.cloned.1.call-start = ((), (), s32[]{:S(2)}) async-start(), calls=%async_computation.1 | async-start | bytes 8912896 | tf_op jit(solution)/shard_map/all_gather | solution.py:20
  146.2 7.2 %copy-start.4 = (bf16[1536,512]{1,0:T(8,128)(2,1)S(1)}, bf16[1536,512]{1,0:T(8,128)(2,1)}, u32[]{:S(2)}) copy-start(bf16[1536,512]{1,0:T(8,128)(2,1)} %all-gather.4.cloned.1.call-done) | copy-start | bytes 4718596
  147.1 6.4 %collective-permute-start = (bf16[3,512]{1,0:T(4,128)(2,1)S(1)}, bf16[3,512]{1,0:T(4,128)(2,1)S(1)}, u32[]{:S(2)}, u32[]{:S(2)}) collective-permute-start(bf16[3,512]{1,0:T(4,128)(2,1)S(1)} %slice.108), channel_id=1, source_target_pairs={{0,32},{32,64},{64,96},{96,128},{128,160},{160,192},{192,224},{224... | collective-permute-start | bytes 9224 | tf_op jit(solution)/shard_map/ppermute | solution.py:15
  151.6 2.3 copy-start.5
  156.1 4.3 %copy-start.1 = (f32[6,4,128,256]{3,2,1,0:T(8,128)S(1)}, f32[6,4,128,256]{3,2,1,0:T(8,128)}, u32[]{:S(2)}) copy-start(f32[6,4,128,256]{3,2,1,0:T(8,128)} %broadcast_dynamic-update-slice_fusion) | copy-start | bytes 9437188
  162.0 1.8 copy-start.2
  264.1 1.9 copy-start.3
  264.1 1.9 copy-start.7
  271.3 2.1 copy-start
  273.3 67.6 %copy-start.6 = (f32[512]{0:T(512)S(1)}, f32[512]{0:T(512)}, u32[]{:S(2)}) copy-start(f32[512]{0:T(512)} %param.19) | copy-start | bytes 6148
Sparse Core Ops, SparseCore 0:
  9.4 136.7 all-gather.3
  163.9 82.4 all-gather.5
where the time goes:
time: 352 us; the launch traced here: 351 us
  waiting for transfers between devices  177 us (50%)
  blocking collectives  93.9 us (27%)
  other arithmetic  34.8 us (10%)
  matrix products  17.5 us (5%)
  between operations  14.4 us (4%)
  local copies, waits for them, and re-layouts  11.6 us (3%)
    all_gather x1, waiting for transfers between devices, on_device(): gathered = lax.all_gather(bc_raw, 'head', axis=0, tiled=True)  128 us
    psum x1, blocking collectives, on_device(): square_sum = lax.psum(jnp.sum(gated_out * gated_out, axis=1), 'head')  66.5 us
    all_gather x1, waiting for transfers between devices, prefix(): gathered = jax.tree.map(lambda a: lax.all_gather(a, axis), part)  46.5 us
    unnamed x1, blocking collectives  27.4 us
    add x14, other arithmetic, combine(): jnp.exp(later[0])[:, None, None] * earlier[1] + later[1]  16.8 us
    another operation x3, other arithmetic  7.34 us
  transfers between devices with their start and end apart: 3, of which 3 were waited for; matrix products, arithmetic and copies ran while one was open for 6% of the time, Pallas kernels for 0%

commit v1 on v0

v1 whole, which is shorter than its diff:
```python
import jax
import jax.numpy as jnp
from jax import lax
from jax.experimental import pallas as pl
from jax.experimental.pallas import tpu as pltpu
from jax.sharding import PartitionSpec as P

HEAD_DIM = 128
STATE = 256
BLOCK = 256
INNER = 16384
NSEQ = 16
NZ = 16
VMEM_SPEC = pl.BlockSpec(memory_space=pltpu.VMEM)
SMEM_SPEC = pl.BlockSpec(memory_space=pltpu.SMEM)
F32 = jnp.float32
BF16 = jnp.bfloat16


def remote(src, dst, send, recv, **where):
    return pltpu.make_async_remote_copy(
        src_ref=src,
        dst_ref=dst,
        send_sem=send,
        recv_sem=recv,
        device_id=where,
        device_id_type=pl.DeviceIdType.MESH,
    )


def greet(targets):
    barrier = pltpu.get_barrier_semaphore()
    for where in targets:
        pl.semaphore_signal(
            barrier, inc=1, device_id=where, device_id_type=pl.DeviceIdType.MESH
        )
    pl.semaphore_wait(barrier, len(targets))


def gather_kernel(raw, out, rim, zsend, zrecv, ysend, yrecv, tsend, trecv, lsem, rsend, rrecv):
    seq = lax.axis_index("seq")
    head = lax.axis_index("head")
    z = head // 2
    yl = head % 2
    right = ((z + 1) % NZ) * 2 + yl
    left = ((z + NZ - 1) % NZ) * 2 + yl
    mate = z * 2 + 1 - yl
    after = (seq + 1) % NSEQ
    before = (seq + NSEQ - 1) % NSEQ
    greet([{"head": right}, {"head": left}, {"head": mate}, {"seq": after}, {"seq": before}])
    sides = (right, left)

    def window(turn):
        return pl.multiple_of(32 * yl + 16 * (turn + yl * (3 - 2 * turn)), 16)

    def span(start, size):
        return pl.ds(pl.multiple_of(start, 16), size)

    def ring(side, step, turn, slot, src):
        return remote(
            src,
            out.at[slot, span(window(turn), 16)],
            zsend.at[side, step, turn],
            zrecv.at[side, step, turn],
            head=sides[side],
        )

    def across(index, slot, src):
        return remote(
            src,
            out.at[slot, span(64 * yl, 32)],
            ysend.at[index],
            yrecv.at[index],
            head=mate,
        )

    sent = []

    def go(copy):
        copy.start()
        sent.append(copy)

    middle = remote(
        raw.at[span(32 - 32 * yl, 16)],
        out.at[z, span(32 + 16 * yl, 16)],
        tsend,
        trecv,
        head=mate,
    )
    go(middle)
    for turn in range(3):
        for side in range(2):
            go(ring(side, 0, turn, z, raw.at[span(window(turn) - 48 * yl, 16)]))
    go(across(0, z, raw.at[span(16 * yl, 32)]))
    own = pltpu.make_async_copy(raw, out.at[z, span(48 * yl, 48)], lsem)
    own.start()
    remote(
        raw.at[span(32 - 32 * yl, 16)],
        out.at[z, span(48 - 16 * yl, 16)],
        tsend,
        trecv,
        head=mate,
    ).wait_recv()
    for side in range(2):
        go(ring(side, 0, 3, z, out.at[z, span(window(3), 16)]))
    for step in range(1, 9):
        slots = ((z + NZ - step) % NZ, (z + step) % NZ)
        for turn in range(4):
            for side in range(2):
                if step == 8 and side != turn // 2:
                    continue
                slot = slots[side]
                piece = out.at[slot, span(window(turn), 16)]
                ring(side, step - 1, turn, slot, piece).wait_recv()
                if step < 7 or (step == 7 and side == turn // 2):
                    go(ring(side, step, turn, slot, piece))
                if turn == 1:
                    index = step + 8 * side
                    go(across(index, slot, out.at[slot, span(64 * yl, 32)]))
    for index in range(16):
        slot = (z + NZ - index) % NZ if index <= 8 else (z + index - 8) % NZ
        landed = out.at[slot, span(64 * (1 - yl), 32)]
        remote(landed, landed, ysend.at[index], yrecv.at[index], head=mate).wait_recv()
    own.wait()
    edge = remote(out.at[NZ - 1, pl.ds(80, 16)], rim, rsend, rrecv, seq=after)
    edge.start()
    for copy in sent:
        copy.wait_send()
    edge.wait()


def gather(raw):
    rows, width = raw.shape
    return pl.pallas_call(
        gather_kernel,
        out_shape=(
            jax.ShapeDtypeStruct((NZ, 2 * rows, width), raw.dtype),
            jax.ShapeDtypeStruct((16, width), raw.dtype),
        ),
        in_specs=[VMEM_SPEC],
        out_specs=(VMEM_SPEC, VMEM_SPEC),
        scratch_shapes=[
            pltpu.SemaphoreType.DMA((2, 8, 4)),
            pltpu.SemaphoreType.DMA((2, 8, 4)),
            pltpu.SemaphoreType.DMA((16,)),
            pltpu.SemaphoreType.DMA((16,)),
            pltpu.SemaphoreType.DMA,
            pltpu.SemaphoreType.DMA,
            pltpu.SemaphoreType.DMA,
            pltpu.SemaphoreType.DMA,
            pltpu.SemaphoreType.DMA,
        ],
        compiler_params=pltpu.CompilerParams(collective_id=0, has_side_effects=True),
        name="gather_bc",
    )(raw)


def split(value):
    high = value.astype(BF16)
    return high, (value - high.astype(F32)).astype(BF16)


def dot(a, b, ca, cb):
    return lax.dot_general(a, b, (((ca,), (cb,)), ((), ())), preferred_element_type=F32)


def spread_heads(column):
    rows = column.shape[0]
    return jnp.concatenate(
        [jnp.broadcast_to(column[:, h : h + 1], (rows, HEAD_DIM)) for h in range(4)], axis=1
    )


def state_step(x, b_in, cum, offset, state):
    last = cum[:, BLOCK - 1 : BLOCK]
    tail = jnp.exp(jnp.transpose(last - offset))
    weighted = x.astype(F32) * spread_heads(tail)
    high, low = split(weighted)
    decay = spread_heads(jnp.transpose(jnp.exp(jnp.broadcast_to(last, (8, 128)))))[0:1]
    return decay * state + dot(b_in, high, 0, 0) + dot(b_in, low, 0, 0), last


def local_kernel(
    a_log, raw, rim, conv_weight, conv_bias, dt, x, act, cum_out, offset_out, message, padded, state, total
):
    block = pl.program_id(0)

    @pl.when(block == 0)
    def _():
        first = lax.axis_index("seq") == 0
        before = rim[...].astype(F32)[8:16, :]
        padded[0:8, :] = jnp.where(first, 0.0, before)
        state[...] = jnp.zeros_like(state)
        total[...] = jnp.zeros_like(total)

    padded[8 : 8 + BLOCK, :] = raw[...].astype(F32)
    summed = jnp.broadcast_to(conv_bias[...], (BLOCK, 2 * STATE))
    for tap in range(4):
        summed = summed + conv_weight[tap : tap + 1, :] * padded[5 + tap : 5 + tap + BLOCK, :]
    acted = jax.nn.silu(summed).astype(BF16)
    act[...] = acted
    padded[0:8, :] = padded[BLOCK : BLOCK + 8, :]

    sub = lax.broadcasted_iota(jnp.int32, (8, BLOCK), 0)
    rate = jnp.full((8, BLOCK), a_log[0], F32)
    for h in range(1, 4):
        rate = jnp.where(sub == h, a_log[h], rate)
    raw_dt = dt[...]
    size = jnp.maximum(raw_dt, 0.0) + jnp.log1p(jnp.exp(-jnp.abs(raw_dt)))
    log_step = -jnp.exp(rate) * size
    row = lax.broadcasted_iota(jnp.int32, (BLOCK, BLOCK), 0)
    column = lax.broadcasted_iota(jnp.int32, (BLOCK, BLOCK), 1)
    upper = jnp.where(row <= column, 1.0, 0.0).astype(BF16)
    high, rest = log_step.astype(BF16), None
    rest = log_step - high.astype(F32)
    middle, low = split(rest)
    cum = (dot(low, upper, 1, 0) + dot(middle, upper, 1, 0)) + dot(high, upper, 1, 0)
    offset = cum - jnp.log(size)
    cum_out[...] = cum
    offset_out[...] = offset
    fresh, last = state_step(x[...], acted[:, :STATE], cum, offset, state[...])
    state[...] = fresh
    total[...] = total[...] + jnp.broadcast_to(last, (8, 128))

    @pl.when(block == pl.num_programs(0) - 1)
    def _():
        gone = spread_heads(jnp.transpose(jnp.exp(total[...])))[0:8]
        for k in range(NSEQ):
            message[k, 0:16, :] = state[16 * k : 16 * k + 16, :]
            message[k, 16:24, :] = gone


def local_states(raw, rim, conv_weight, conv_bias, dt, a_log, x):
    length, width = x.shape
    blocks = length // BLOCK
    by_row = lambda b: (b, 0)
    by_lane = lambda b: (0, b)
    fixed = lambda b: (0, 0)
    return pl.pallas_call(
        local_kernel,
        grid=(blocks,),
        out_shape=(
            jax.ShapeDtypeStruct((length, 2 * STATE), BF16),
            jax.ShapeDtypeStruct((8, length), F32),
            jax.ShapeDtypeStruct((8, length), F32),
            jax.ShapeDtypeStruct((NSEQ, 24, width), F32),
        ),
        in_specs=[
            SMEM_SPEC,
            pl.BlockSpec((BLOCK, 2 * STATE), by_row),
            pl.BlockSpec((16, 2 * STATE), fixed),
            pl.BlockSpec((4, 2 * STATE), fixed),
            pl.BlockSpec((1, 2 * STATE), fixed),
            pl.BlockSpec((8, BLOCK), by_lane),
            pl.BlockSpec((BLOCK, width), by_row),
        ],
        out_specs=(
            pl.BlockSpec((BLOCK, 2 * STATE), by_row),
            pl.BlockSpec((8, BLOCK), by_lane),
            pl.BlockSpec((8, BLOCK), by_lane),
            pl.BlockSpec((NSEQ, 24, width), lambda b: (0, 0, 0)),
        ),
        scratch_shapes=[
            pltpu.VMEM((BLOCK + 8, 2 * STATE), F32),
            pltpu.VMEM((STATE, width), F32),
            pltpu.VMEM((8, 128), F32),
        ],
        name="local_states",
    )(a_log, raw, rim, conv_weight, conv_bias, dt, x)


def scan_kernel(message, out, landed, prefix, asend, arecv, bsend, brecv):
    me = lax.axis_index("seq")
    others = [(me + hop) % NSEQ for hop in range(1, NSEQ)]
    greet([{"seq": other} for other in others])
    sent = []
    for other in others:
        copy = remote(message.at[other], landed.at[me], asend.at[other], arecv.at[me], seq=other)
        copy.start()
        sent.append(copy)
    landed[me] = message[me]
    for other in others:
        remote(
            landed.at[other], landed.at[other], asend.at[other], arecv.at[other], seq=other
        ).wait_recv()
    state = jnp.zeros(prefix.shape[1:], F32)
    for s in range(NSEQ):
        prefix[s] = state
        if s < NSEQ - 1:
            state = landed[s, 16:17, :] * state + landed[s, 0:16, :]
    for other in others:
        copy = remote(prefix.at[other], out.at[me], bsend.at[other], brecv.at[me], seq=other)
        copy.start()
        sent.append(copy)
    out[me] = prefix[me]
    for other in others:
        remote(
            out.at[other], out.at[other], bsend.at[other], brecv.at[other], seq=other
        ).wait_recv()
    for copy in sent:
        copy.wait_send()


def incoming_state(message):
    slices, rows, width = message.shape
    return pl.pallas_call(
        scan_kernel,
        out_shape=jax.ShapeDtypeStruct((slices, 16, width), F32),
        in_specs=[VMEM_SPEC],
        out_specs=VMEM_SPEC,
        scratch_shapes=[
            pltpu.VMEM((slices, rows, width), F32),
            pltpu.VMEM((slices, 16, width), F32),
        ]
        + [pltpu.SemaphoreType.DMA((slices,))] * 4,
        compiler_params=pltpu.CompilerParams(collective_id=1, has_side_effects=True),
        name="scan_states",
    )(message)


def mix_kernel(d_skip, act, cum_ref, offset_ref, entry, x_ref, z_ref, gated, squares, state):
    block = pl.program_id(0)

    @pl.when(block == 0)
    def _():
        state[...] = entry[...]
        squares[...] = jnp.zeros_like(squares)

    b_in = act[:, :STATE]
    c_out = act[:, STATE:]
    x = x_ref[...]
    cum = cum_ref[...]
    offset = offset_ref[...]
    gram = dot(c_out, b_in, 1, 1)
    high, low = split(state[...])
    carried = dot(c_out, high, 1, 0) + dot(c_out, low, 1, 0)
    cum_column = jnp.transpose(cum)
    row = lax.broadcasted_iota(jnp.int32, (BLOCK, BLOCK), 0)
    column = lax.broadcasted_iota(jnp.int32, (BLOCK, BLOCK), 1)
    causal = row >= column
    for h in range(4):
        lanes = slice(h * HEAD_DIM, (h + 1) * HEAD_DIM)
        at = cum_column[:, h : h + 1]
        decay = jnp.exp(jnp.where(causal, at - offset[h : h + 1, :], -1e30))
        weights = (gram * decay).astype(BF16)
        x_head = x[:, lanes]
        out = dot(weights, x_head, 1, 0) + jnp.exp(at) * carried[:, lanes]
        out = out + d_skip[h] * x_head.astype(F32)
        out = out * jax.nn.silu(z_ref[:, lanes].astype(F32))
        gated[:, lanes] = out
    full = gated[...]
    sums = dot(jnp.ones((8, full.shape[1]), BF16), (full * full).astype(BF16), 1, 1)
    squares[pl.ds(2 * block, 1), :] = sums[0:1, 0:128]
    squares[pl.ds(2 * block + 1, 1), :] = sums[0:1, 128:256]
    state[...] = state_step(x, b_in, cum, offset, state[...])[0]


def mix(act, cum, offset, entry, x, z_gate, d_skip):
    length, width = x.shape
    by_row = lambda b: (b, 0)
    by_lane = lambda b: (0, b)
    fixed = lambda b: (0, 0)
    return pl.pallas_call(
        mix_kernel,
        grid=(length // BLOCK,),
        out_shape=(
            jax.ShapeDtypeStruct((length, width), F32),
            jax.ShapeDtypeStruct((16, 128), F32),
        ),
        in_specs=[
            SMEM_SPEC,
            pl.BlockSpec((BLOCK, 2 * STATE), by_row),
            pl.BlockSpec((8, BLOCK), by_lane),
            pl.BlockSpec((8, BLOCK), by_lane),
            pl.BlockSpec((STATE, width), fixed),
            pl.BlockSpec((BLOCK, width), by_row),
            pl.BlockSpec((BLOCK, width), by_row),
        ],
        out_specs=(pl.BlockSpec((BLOCK, width), by_row), pl.BlockSpec((16, 128), fixed)),
        scratch_shapes=[pltpu.VMEM((STATE, width), F32)],
        name="mix",
    )(d_skip, act, cum, offset, entry, x, z_gate)


def sum_kernel(part, out, pair, landed, psend, precv, zsend, zrecv):
    head = lax.axis_index("head")
    z = head // 2
    yl = head % 2
    mate = z * 2 + 1 - yl
    hops = (8, 7, 9, 6, 10, 5, 11, 4, 12, 3, 13, 2, 14, 1, 15)
    places = [(z + hop) % NZ for hop in hops]
    greet([{"head": mate}] + [{"head": place * 2 + yl} for place in places])
    first = remote(part, pair, psend, precv, head=mate)
    first.start()
    first.wait()
    landed[z] = part[...] + pair[...]
    sent = []
    for place in places:
        copy = remote(
            landed.at[z], landed.at[z], zsend.at[place], zrecv.at[z], head=place * 2 + yl
        )
        copy.start()
        sent.append(copy)
    for place in reversed(places):
        remote(
            landed.at[place],
            landed.at[place],
            zsend.at[place],
            zrecv.at[place],
            head=place * 2 + yl,
        ).wait_recv()
    total = landed[0]
    for k in range(1, NZ):
        total = total + landed[k]
    out[...] = total
    for copy in sent:
        copy.wait_send()


def sum_squares(part):
    return pl.pallas_call(
        sum_kernel,
        out_shape=jax.ShapeDtypeStruct(part.shape, F32),
        in_specs=[VMEM_SPEC],
        out_specs=VMEM_SPEC,
        scratch_shapes=[
            pltpu.VMEM(part.shape, F32),
            pltpu.VMEM((NZ,) + part.shape, F32),
            pltpu.SemaphoreType.DMA,
            pltpu.SemaphoreType.DMA,
            pltpu.SemaphoreType.DMA((NZ,)),
            pltpu.SemaphoreType.DMA((NZ,)),
        ],
        compiler_params=pltpu.CompilerParams(collective_id=2, has_side_effects=True),
        name="sum_squares",
    )(part)


def norm_kernel(squares, gain, gated, out):
    block = pl.program_id(0)
    for half in range(2):
        total = squares[pl.ds(2 * block + half, 1), :]
        inverse = lax.rsqrt(total / INNER + 1e-05)
        column = jnp.transpose(jnp.broadcast_to(inverse, (8, 128)))[:, 0:1]
        rows = slice(128 * half, 128 * half + 128)
        out[rows, :] = (gated[rows, :] * column * gain[...]).astype(BF16)


def norm(squares, gain, gated):
    length, width = gated.shape
    return pl.pallas_call(
        norm_kernel,
        grid=(length // BLOCK,),
        out_shape=jax.ShapeDtypeStruct((length, width), BF16),
        in_specs=[
            pl.BlockSpec((16, 128), lambda b: (0, 0)),
            pl.BlockSpec((1, width), lambda b: (0, 0)),
            pl.BlockSpec((BLOCK, width), lambda b: (b, 0)),
        ],
        out_specs=pl.BlockSpec((BLOCK, width), lambda b: (b, 0)),
        name="norm",
    )(squares, gain, gated)


def on_device(x_inner, z_gate, bc_raw, conv_weight, conv_bias, dt_raw, a_log, d_skip, norm_gain):
    dt = jnp.pad(dt_raw.T, ((0, 4), (0, 0)))
    gathered, rim = gather(bc_raw)
    raw = gathered.reshape(x_inner.shape[0], 2 * STATE)
    act, cum, offset, message = local_states(
        raw, rim, conv_weight, conv_bias[None, :], dt, a_log, x_inner
    )
    entry = incoming_state(message).reshape(STATE, x_inner.shape[1])
    gated, squares = mix(act, cum, offset, entry, x_inner, z_gate, d_skip)
    return norm(sum_squares(squares), norm_gain[None, :], gated)


def solution(mesh):
    placed = (
        P("seq", "head"),
        P("seq", "head"),
        P(("seq", "head"), None),
        P(),
        P(),
        P("seq", "head"),
        P("head"),
        P("head"),
        P("head"),
    )
    return jax.shard_map(
        on_device, mesh=mesh, in_specs=placed, out_specs=P("seq", "head"), check_vma=False
    )
```

time: 352 us -> 119 us (0.34)
  the two profiles are of different devices: /device:TPU:22 before, /device:TPU:16 now
where the time goes in v1:
time: 119 us; the launch traced here: 118 us
  Pallas kernels  117 us (98%)
  local copies, waits for them, and re-layouts  1.37 us (1%)
    pallas_call x1, Pallas kernels, gather(): pl.pallas_call(gather_kernel, out_shape=(jax.ShapeDtypeStruct((NZ, 2 * ro...  42.5 us
    pallas_call x1, Pallas kernels, incoming_state(): pl.pallas_call(scan_kernel, out_shape=jax.ShapeDtypeStruct((slices, 16, w...  29.7 us
    pallas_call x1, Pallas kernels, sum_squares(): pl.pallas_call(sum_kernel, out_shape=jax.ShapeDtypeStruct(part.shape, F32...  19 us
    pallas_call x1, Pallas kernels, mix(): pl.pallas_call(mix_kernel, grid=(length // BLOCK,), out_shape=(jax.ShapeD...  10.8 us
    pallas_call x1, Pallas kernels, local_states(): pl.pallas_call(local_kernel, grid=(blocks,), out_shape=(jax.ShapeDtypeStr...  9.41 us
    pallas_call x1, Pallas kernels, norm(): pl.pallas_call(norm_kernel, grid=(length // BLOCK,), out_shape=jax.ShapeD...  5.36 us

profile of v1, /device:TPU:16, one launch (start us, length us, event | category | flops | bytes accessed | tf_op | source)
XLA Modules:
  0.0 118.1 jit_solution(2728976476146098669)
XLA Ops:
  0.0 1.4 %pad.4.dt = f32[8,1536]{1,0:T(8,128)} pad(f32[4,1536]{1,0:T(4,128)} %bitcast.7, f32[]{:T(128)} %constant.2.clone.1), padding=0_4x0_0 | pad | bytes 73732 | tf_op jit(solution)/shard_map/jit(_pad)/pad | solution.py:466
  1.4 42.5 %gather_bc.1 = (bf16[16,96,512]{2,1,0:T(8,128)(2,1)}, bf16[16,512]{1,0:T(8,128)(2,1)}) custom-call(bf16[48,512]{1,0:T(8,128)(2,1)} %raw.1), custom_call_target="tpu_custom_call" | custom-call | tf_op jit(solution)/shard_map/gather_bc/pallas_call | solution.py:134
  43.9 9.4 %local_states.1 = (bf16[1536,512]{1,0:T(8,128)(2,1)}, f32[8,1536]{1,0:T(8,128)}, f32[8,1536]{1,0:T(8,128)}, f32[16,24,512]{2,1,0:T(8,128)}) custom-call(f32[4]{0:T(128)} %a_log.1, bf16[1536,512]{1,0:T(8,128)(2,1)} %bitcast.6, bf16[16,512]{1,0:T(8,128)(2,1)} %get-tuple-element.14.rim, f32[4,512]{1,0:T(4,128)} %conv_weight.1, f32[1,512]{1,0:T(1,128)} %bitcast.8, ...), custom_call_target="tpu_custom_call" | custom-call | tf_op jit(solution)/shard_map/local_states/pallas_call | solution.py:239
  53.3 29.7 %scan_states.1 = f32[16,16,512]{2,1,0:T(8,128)} custom-call(f32[16,24,512]{2,1,0:T(8,128)} %get-tuple-element.18.message), custom_call_target="tpu_custom_call" | custom-call | tf_op jit(solution)/shard_map/scan_states/pallas_call | solution.py:306
  83.0 10.8 %mix.1 = (f32[1536,512]{1,0:T(8,128)}, f32[16,128]{1,0:T(8,128)}) custom-call(f32[4]{0:T(128)} %d_skip.1, bf16[1536,512]{1,0:T(8,128)(2,1)} %get-tuple-element.15.act, f32[8,1536]{1,0:T(8,128)} %get-tuple-element.16.cum_ref, f32[8,1536]{1,0:T(8,128)} %get-tuple-element.17.offset_ref, f32[256,512]{1,0:T(8,128)} %bitcast.5, bf16[1536,512]{1,0:T(8,128)(2,1)} %x_ref.1, ...), custom_call_target="tpu_custom_call" | custom-call | tf_op jit(solution)/shard_map/mix/pallas_call | solution.py:363
  93.8 19.0 %sum_squares.1.squares = f32[16,128]{1,0:T(8,128)} custom-call(f32[16,128]{1,0:T(8,128)} %get-tuple-element.19.part), custom_call_target="tpu_custom_call" | custom-call | tf_op jit(solution)/shard_map/sum_squares/pallas_call | solution.py:421
  112.8 5.4 %norm.1 = bf16[1536,512]{1,0:T(8,128)(2,1)} custom-call(f32[16,128]{1,0:T(8,128)} %sum_squares.1.squares, f32[1,512]{1,0:T(1,128)} %bitcast.9, f32[1536,512]{1,0:T(8,128)} %get-tuple-element.20.gated), custom_call_target="tpu_custom_call" | custom-call | tf_op jit(solution)/shard_map/norm/pallas_call | solution.py:451

commit v2 on v1

v2 whole, which is shorter than its diff:
```python
import jax
import jax.numpy as jnp
from jax import lax
from jax.experimental import pallas as pl
from jax.experimental.pallas import tpu as pltpu
from jax.sharding import PartitionSpec as P

HEAD_DIM = 128
STATE = 256
BLOCK = 256
INNER = 16384
NSEQ = 16
NZ = 16
VMEM_SPEC = pl.BlockSpec(memory_space=pltpu.VMEM)
SMEM_SPEC = pl.BlockSpec(memory_space=pltpu.SMEM)
F32 = jnp.float32
BF16 = jnp.bfloat16


def remote(src, dst, send, recv, **where):
    return pltpu.make_async_remote_copy(
        src_ref=src,
        dst_ref=dst,
        send_sem=send,
        recv_sem=recv,
        device_id=where,
        device_id_type=pl.DeviceIdType.MESH,
    )


def greet(targets):
    barrier = pltpu.get_barrier_semaphore()
    for where in targets:
        pl.semaphore_signal(
            barrier, inc=1, device_id=where, device_id_type=pl.DeviceIdType.MESH
        )
    pl.semaphore_wait(barrier, len(targets))


def gather_kernel(raw, out, rim, zsend, zrecv, ysend, yrecv, tsend, trecv, lsem, rsend, rrecv):
    seq = lax.axis_index("seq")
    head = lax.axis_index("head")
    z = head // 2
    yl = head % 2
    right = ((z + 1) % NZ) * 2 + yl
    left = ((z + NZ - 1) % NZ) * 2 + yl
    mate = z * 2 + 1 - yl
    after = (seq + 1) % NSEQ
    before = (seq + NSEQ - 1) % NSEQ
    greet([{"head": right}, {"head": left}, {"head": mate}, {"seq": after}, {"seq": before}])
    sides = (right, left)

    def window(turn):
        return pl.multiple_of(32 * yl + 16 * (turn + yl * (3 - 2 * turn)), 16)

    def span(start, size):
        return pl.ds(pl.multiple_of(start, 16), size)

    def ring(side, step, turn, slot, src):
        return remote(
            src,
            out.at[slot, span(window(turn), 16)],
            zsend.at[side, step, turn],
            zrecv.at[side, step, turn],
            head=sides[side],
        )

    def across(index, slot, src):
        return remote(
            src,
            out.at[slot, span(64 * yl, 32)],
            ysend.at[index],
            yrecv.at[index],
            head=mate,
        )

    sent = []

    def go(copy):
        copy.start()
        sent.append(copy)

    middle = remote(
        raw.at[span(32 - 32 * yl, 16)],
        out.at[z, span(32 + 16 * yl, 16)],
        tsend,
        trecv,
        head=mate,
    )
    go(middle)
    for turn in range(3):
        for side in range(2):
            go(ring(side, 0, turn, z, raw.at[span(window(turn) - 48 * yl, 16)]))
    go(across(0, z, raw.at[span(16 * yl, 32)]))
    own = pltpu.make_async_copy(raw, out.at[z, span(48 * yl, 48)], lsem)
    own.start()
    remote(
        raw.at[span(32 - 32 * yl, 16)],
        out.at[z, span(48 - 16 * yl, 16)],
        tsend,
        trecv,
        head=mate,
    ).wait_recv()
    for side in range(2):
        go(ring(side, 0, 3, z, out.at[z, span(window(3), 16)]))
    for step in range(1, 9):
        slots = ((z + NZ - step) % NZ, (z + step) % NZ)
        for turn in range(4):
            for side in range(2):
                if step == 8 and side != turn // 2:
                    continue
                slot = slots[side]
                piece = out.at[slot, span(window(turn), 16)]
                ring(side, step - 1, turn, slot, piece).wait_recv()
                if step < 7 or (step == 7 and side == turn // 2):
                    go(ring(side, step, turn, slot, piece))
                if turn == 1:
                    index = step + 8 * side
                    go(across(index, slot, out.at[slot, span(64 * yl, 32)]))
    for index in range(16):
        slot = (z + NZ - index) % NZ if index <= 8 else (z + index - 8) % NZ
        landed = out.at[slot, span(64 * (1 - yl), 32)]
        remote(landed, landed, ysend.at[index], yrecv.at[index], head=mate).wait_recv()
    own.wait()
    edge = remote(out.at[NZ - 1, pl.ds(80, 16)], rim, rsend, rrecv, seq=after)
    edge.start()
    for copy in sent:
        copy.wait_send()
    edge.wait()


def gather(raw):
    rows, width = raw.shape
    return pl.pallas_call(
        gather_kernel,
        out_shape=(
            jax.ShapeDtypeStruct((NZ, 2 * rows, width), raw.dtype),
            jax.ShapeDtypeStruct((16, width), raw.dtype),
        ),
        in_specs=[VMEM_SPEC],
        out_specs=(VMEM_SPEC, VMEM_SPEC),
        scratch_shapes=[
            pltpu.SemaphoreType.DMA((2, 8, 4)),
            pltpu.SemaphoreType.DMA((2, 8, 4)),
            pltpu.SemaphoreType.DMA((16,)),
            pltpu.SemaphoreType.DMA((16,)),
            pltpu.SemaphoreType.DMA,
            pltpu.SemaphoreType.DMA,
            pltpu.SemaphoreType.DMA,
            pltpu.SemaphoreType.DMA,
            pltpu.SemaphoreType.DMA,
        ],
        compiler_params=pltpu.CompilerParams(collective_id=0, has_side_effects=True),
        name="gather_bc",
    )(raw)


def split(value):
    high = value.astype(BF16)
    return high, (value - high.astype(F32)).astype(BF16)


def dot(a, b, ca, cb):
    return lax.dot_general(a, b, (((ca,), (cb,)), ((), ())), preferred_element_type=F32)


def spread_heads(column):
    rows = column.shape[0]
    return jnp.concatenate(
        [jnp.broadcast_to(column[:, h : h + 1], (rows, HEAD_DIM)) for h in range(4)], axis=1
    )


def lane_row(tile):
    return jnp.concatenate([tile[h : h + 1, :] for h in range(4)], axis=1)


def mixer_kernel(
    a_log,
    d_skip,
    raw,
    rim,
    conv_weight,
    conv_bias,
    dt,
    gain,
    x_far,
    z_far,
    out,
    x_ref,
    z_ref,
    act,
    padded,
    cums,
    offsets,
    starts,
    priors,
    state,
    total,
    mixed,
    message,
    fade,
    landed,
    fades,
    prefix,
    entry,
    squares,
    pair,
    parts,
    local_sem,
    fsend,
    frecv,
    asend,
    arecv,
    bsend,
    brecv,
    psend,
    precv,
    zsend,
    zrecv,
):
    seq = lax.axis_index("seq")
    head = lax.axis_index("head")
    z = head // 2
    yl = head % 2
    mate = z * 2 + 1 - yl
    blocks = x_ref.shape[0] // BLOCK
    others = [(seq + hop) % NSEQ for hop in (10, 6, 14, 11, 9, 5, 13, 7, 15, 3, 8, 12, 4, 2, 1)]
    hops = (8, 7, 9, 6, 10, 5, 11, 4, 12, 3, 13, 2, 14, 1, 15)
    places = [(z + hop) % NZ for hop in hops]
    targets = [{"seq": other} for other in others] + [{"head": mate}]
    targets = targets + [{"head": place * 2 + yl} for place in places]
    barrier = pltpu.get_barrier_semaphore()
    for where in targets:
        pl.semaphore_signal(
            barrier, inc=1, device_id=where, device_id_type=pl.DeviceIdType.MESH
        )
    fetch_x = pltpu.make_async_copy(x_far, x_ref, local_sem.at[0])
    fetch_z = pltpu.make_async_copy(z_far, z_ref, local_sem.at[1])
    fetch_x.start()
    fetch_z.start()

    def rows_of(block):
        return pl.ds(pl.multiple_of(block * BLOCK, BLOCK), BLOCK)

    sub = lax.broadcasted_iota(jnp.int32, (8, BLOCK), 0)
    rate = jnp.full((8, BLOCK), a_log[0], F32)
    for h in range(1, 4):
        rate = jnp.where(sub == h, a_log[h], rate)
    rate = -jnp.exp(rate)
    row = lax.broadcasted_iota(jnp.int32, (BLOCK, BLOCK), 0)
    column = lax.broadcasted_iota(jnp.int32, (BLOCK, BLOCK), 1)
    upper = jnp.where(row <= column, 1.0, 0.0).astype(BF16)
    padded[0:8, :] = jnp.where(seq == 0, 0.0, rim[...].astype(F32)[8:16, :])
    state[...] = jnp.zeros_like(state)
    total[...] = jnp.zeros_like(total)
    squares[...] = jnp.zeros_like(squares)
    fetch_x.wait()

    def first_pass(block, _):
        rows = rows_of(block)
        padded[8 : 8 + BLOCK, :] = raw[rows, :].astype(F32)
        summed = jnp.broadcast_to(conv_bias[...], (BLOCK, 2 * STATE))
        for tap in range(4):
            summed = summed + conv_weight[tap : tap + 1, :] * padded[5 + tap : 5 + tap + BLOCK, :]
        acted = jax.nn.silu(summed).astype(BF16)
        act[rows, :] = acted
        padded[0:8, :] = padded[BLOCK : BLOCK + 8, :]
        raw_dt = dt[block]
        size = jnp.maximum(raw_dt, 0.0) + jnp.log1p(jnp.exp(-jnp.abs(raw_dt)))
        log_step = rate * size
        high = log_step.astype(BF16)
        middle, low = split(log_step - high.astype(F32))
        cum = (dot(low, upper, 1, 0) + dot(middle, upper, 1, 0)) + dot(high, upper, 1, 0)
        offset = cum - jnp.log(size)
        cums[block] = cum
        offsets[block] = offset
        last = cum[:, BLOCK - 1 : BLOCK]
        tail = jnp.exp(jnp.transpose(last - offset))
        high, low = split(x_ref[rows, :].astype(F32) * spread_heads(tail))
        b_in = acted[:, :STATE]
        ends = jnp.broadcast_to(last, (8, 128))
        starts[block] = state[...]
        priors[block] = jnp.exp(total[...])
        fresh = dot(b_in, high, 0, 0) + dot(b_in, low, 0, 0)
        state[...] = lane_row(jnp.exp(ends)) * state[...] + fresh
        total[...] = total[...] + ends
        return 0

    lax.fori_loop(0, blocks, first_pass, 0)
    for k in range(NSEQ):
        message[k] = state[16 * k : 16 * k + 16, :].astype(BF16)
    fade[...] = jnp.exp(total[...])
    pl.semaphore_wait(barrier, len(targets))
    sent = []
    for other in others:
        copy = remote(fade, fades.at[seq], fsend.at[other], frecv.at[seq], seq=other)
        copy.start()
        sent.append(copy)
        copy = remote(message.at[other], landed.at[seq], asend.at[other], arecv.at[seq], seq=other)
        copy.start()
        sent.append(copy)
    landed[seq] = message[seq]
    fades[seq] = fade[...]

    causal = row >= column

    def inner_pass(block, _):
        rows = rows_of(block)
        gram = dot(act[rows, STATE:], act[rows, :STATE], 1, 1)
        at_all = jnp.transpose(cums[block])
        offset = offsets[block]
        for h in range(4):
            lanes = slice(h * HEAD_DIM, (h + 1) * HEAD_DIM)
            gap = at_all[:, h : h + 1] - offset[h : h + 1, :]
            decay = jnp.exp(jnp.where(causal, gap, -1e30))
            x_head = x_ref[rows, lanes]
            mixed[rows, lanes] = dot(
                (gram * decay).astype(BF16), x_head, 1, 0
            ) + d_skip[h] * x_head.astype(F32)
        return 0

    lax.fori_loop(0, blocks // 2, inner_pass, 0)
    for other in others:
        remote(fades.at[other], fades.at[other], fsend.at[other], frecv.at[other], seq=other).wait_recv()
        remote(
            landed.at[other], landed.at[other], asend.at[other], arecv.at[other], seq=other
        ).wait_recv()
    running = jnp.zeros((16, x_ref.shape[1]), F32)
    for s in range(NSEQ):
        prefix[s] = running.astype(BF16)
        if s < NSEQ - 1:
            running = lane_row(fades[s]) * running + landed[s].astype(F32)
    for other in others:
        copy = remote(prefix.at[other], entry.at[seq], bsend.at[other], brecv.at[seq], seq=other)
        copy.start()
        sent.append(copy)
    entry[seq] = prefix[seq]
    lax.fori_loop(blocks // 2, blocks, inner_pass, 0)
    fetch_z.wait()
    for other in others:
        remote(
            entry.at[other], entry.at[other], bsend.at[other], brecv.at[other], seq=other
        ).wait_recv()
    state[...] = entry[...].astype(F32).reshape(state.shape)
    ones = jnp.ones((8, x_ref.shape[1]), BF16)

    def last_pass(block, _):
        rows = rows_of(block)
        high, low = split(starts[block] + lane_row(priors[block]) * state[...])
        c_out = act[rows, STATE:]
        carried = dot(c_out, high, 1, 0) + dot(c_out, low, 1, 0)
        scale = spread_heads(jnp.exp(jnp.transpose(cums[block])))
        gate = jax.nn.silu(z_ref[rows, :].astype(F32))
        gated = (mixed[rows, :] + scale * carried) * gate
        mixed[rows, :] = gated
        sums = dot(ones, (gated * gated).astype(BF16), 1, 1)
        squares[pl.ds(2 * block, 1), :] = sums[0:1, 0:128]
        squares[pl.ds(2 * block + 1, 1), :] = sums[0:1, 128:256]
        return 0

    lax.fori_loop(0, blocks, last_pass, 0)
    first = remote(squares, pair, psend, precv, head=mate)
    first.start()
    first.wait()
    parts[z] = squares[...] + pair[...]
    for place in places:
        copy = remote(
            parts.at[z], parts.at[z], zsend.at[place], zrecv.at[z], head=place * 2 + yl
        )
        copy.start()
        sent.append(copy)
    for place in reversed(places):
        remote(
            parts.at[place], parts.at[place], zsend.at[place], zrecv.at[place], head=place * 2 + yl
        ).wait_recv()
    whole = parts[0]
    for k in range(1, NZ):
        whole = whole + parts[k]
    pair[...] = lax.rsqrt(whole / INNER + 1e-05)

    def norm_pass(part, _):
        rows = pl.ds(pl.multiple_of(part * 128, 128), 128)
        inverse = jnp.transpose(jnp.broadcast_to(pair[pl.ds(part, 1), :], (8, 128)))[:, 0:1]
        out[rows, :] = (mixed[rows, :] * inverse * gain[...]).astype(BF16)
        return 0

    lax.fori_loop(0, 2 * blocks, norm_pass, 0)
    for copy in sent:
        copy.wait_send()


def mixer(raw, rim, conv_weight, conv_bias, dt, a_log, d_skip, gain, x, z_gate):
    length, width = x.shape
    blocks = length // BLOCK
    far = pl.BlockSpec(memory_space=pl.ANY)
    dma = pltpu.SemaphoreType.DMA
    return pl.pallas_call(
        mixer_kernel,
        out_shape=jax.ShapeDtypeStruct((length, width), BF16),
        in_specs=[SMEM_SPEC, SMEM_SPEC] + [VMEM_SPEC] * 6 + [far, far],
        out_specs=VMEM_SPEC,
        scratch_shapes=[
            pltpu.VMEM((length, width), BF16),
            pltpu.VMEM((length, width), BF16),
            pltpu.VMEM((length, 2 * STATE), BF16),
            pltpu.VMEM((BLOCK + 8, 2 * STATE), F32),
            pltpu.VMEM((blocks, 8, BLOCK), F32),
            pltpu.VMEM((blocks, 8, BLOCK), F32),
            pltpu.VMEM((blocks, STATE, width), F32),
            pltpu.VMEM((blocks, 8, 128), F32),
            pltpu.VMEM((STATE, width), F32),
            pltpu.VMEM((8, 128), F32),
            pltpu.VMEM((length, width), F32),
            pltpu.VMEM((NSEQ, 16, width), BF16),
            pltpu.VMEM((8, 128), F32),
            pltpu.VMEM((NSEQ, 16, width), BF16),
            pltpu.VMEM((NSEQ, 8, 128), F32),
            pltpu.VMEM((NSEQ, 16, width), BF16),
            pltpu.VMEM((NSEQ, 16, width), BF16),
            pltpu.VMEM((16, 128), F32),
            pltpu.VMEM((16, 128), F32),
            pltpu.VMEM((NZ, 16, 128), F32),
            dma((2,)),
        ]
        + [dma((NSEQ,))] * 6
        + [dma, dma, dma((NZ,)), dma((NZ,))],
        compiler_params=pltpu.CompilerParams(
            collective_id=1, has_side_effects=True, vmem_limit_bytes=48 * 1024 * 1024
        ),
        name="mixer",
    )(a_log, d_skip, raw, rim, conv_weight, conv_bias, dt, gain, x, z_gate)


def on_device(x_inner, z_gate, bc_raw, conv_weight, conv_bias, dt_raw, a_log, d_skip, norm_gain):
    length = x_inner.shape[0]
    dt = jnp.pad(dt_raw.T, ((0, 4), (0, 0)))
    dt = jnp.transpose(dt.reshape(8, length // BLOCK, BLOCK), (1, 0, 2))
    gathered, rim = gather(bc_raw)
    raw = gathered.reshape(length, 2 * STATE)
    return mixer(
        raw,
        rim,
        conv_weight,
        conv_bias[None, :],
        dt,
        a_log,
        d_skip,
        norm_gain[None, :],
        x_inner,
        z_gate,
    )


def solution(mesh):
    placed = (
        P("seq", "head"),
        P("seq", "head"),
        P(("seq", "head"), None),
        P(),
        P(),
        P("seq", "head"),
        P("head"),
        P("head"),
        P("head"),
    )
    return jax.shard_map(
        on_device, mesh=mesh, in_specs=placed, out_specs=P("seq", "head"), check_vma=False
    )
```

time: 119 us -> 93.7 us (0.79)
  the two profiles are of different devices: /device:TPU:16 before, /device:TPU:8 now
where the time goes in v2:
time: 93.7 us; the launch traced here: 93.2 us
  Pallas kernels  84.4 us (90%)
  local copies, waits for them, and re-layouts  8.78 us (9%)
    pallas_call x1, Pallas kernels, gather(): pl.pallas_call(gather_kernel, out_shape=(jax.ShapeDtypeStruct((NZ, 2 * ro...  45.4 us
    pallas_call x1, Pallas kernels, mixer(): pl.pallas_call(mixer_kernel, out_shape=jax.ShapeDtypeStruct((length, widt...  39 us
    unnamed x17, local copies, waits for them, and re-layouts  8.04 us

profile of v2, /device:TPU:8, one launch (start us, length us, event | category | flops | bytes accessed | tf_op | source)
XLA Modules:
  0.0 93.2 jit_solution(972848477096963741)
XLA Ops:
  0.0 0.7 pad.4
  0.7 45.4 %gather_bc.1 = (bf16[16,96,512]{2,1,0:T(8,128)(2,1)}, bf16[16,512]{1,0:T(8,128)(2,1)}) custom-call(bf16[48,512]{1,0:T(8,128)(2,1)} %raw.1), custom_call_target="tpu_custom_call" | custom-call | tf_op jit(solution)/shard_map/gather_bc/pallas_call | solution.py:134
  46.2 0.0 copy-start
  46.2 1.4 %copy-done = bf16[1536,512]{1,0:T(8,128)(2,1)S(1)} copy-done((bf16[1536,512]{1,0:T(8,128)(2,1)S(1)}, bf16[1536,512]{1,0:T(8,128)(2,1)}, u32[]{:S(2)}) %copy-start) | copy-done | bytes 1572888
  47.6 0.0 copy-start.1
  47.6 1.4 %copy-done.1 = bf16[16,96,512]{2,1,0:T(8,128)(2,1)S(1)} copy-done((bf16[16,96,512]{2,1,0:T(8,128)(2,1)S(1)}, bf16[16,96,512]{2,1,0:T(8,128)(2,1)}, u32[]{:S(2)}) %copy-start.1) | copy-done | bytes 1572888
  49.0 0.0 copy-start.2
  49.0 0.7 copy-done.2
  49.7 0.0 copy-start.3
  49.7 0.7 copy-done.3
  50.4 0.0 copy-start.4
  50.4 0.7 copy-done.4
  51.1 0.0 copy-start.5
  51.1 0.7 copy-done.5
  51.8 0.0 copy-start.6
  51.8 0.7 copy-done.6
  52.4 0.0 copy-start.7
  52.4 0.7 copy-done.7
  53.1 39.0 %mixer.1 = bf16[1536,512]{1,0:T(8,128)(2,1)S(1)} custom-call(f32[4]{0:T(128)S(1)} %copy-done.6, f32[4]{0:T(128)S(1)} %copy-done.7, bf16[1536,512]{1,0:T(8,128)(2,1)S(1)} %bitcast.7, bf16[16,512]{1,0:T(8,128)(2,1)S(1)} %copy-done.2, f32[4,512]{1,0:T(4,128)S(1)} %copy-done.3, f32[1,512]{1,0:T(1,128)S(1)} %bitcast.9, f32[6,8,256]{2,1,0:T(8,128)S(1)} %bitcast.8, ...), custom_call_target="tpu_custom_call" | custom-call | tf_op jit(solution)/shard_map/mixer/pallas_call | solution.py:398
  92.1 1.1 %copy.11 = bf16[1536,512]{1,0:T(8,128)(2,1)} copy(bf16[1536,512]{1,0:T(8,128)(2,1)S(1)} %mixer.1) | data formatting | bytes 3145728
Async XLA Ops:
  46.2 1.4 %copy-start = (bf16[1536,512]{1,0:T(8,128)(2,1)S(1)}, bf16[1536,512]{1,0:T(8,128)(2,1)}, u32[]{:S(2)}) copy-start(bf16[1536,512]{1,0:T(8,128)(2,1)} %x_far.1) | copy-start | bytes 4718596
  47.6 1.4 %copy-start.1 = (bf16[16,96,512]{2,1,0:T(8,128)(2,1)S(1)}, bf16[16,96,512]{2,1,0:T(8,128)(2,1)}, u32[]{:S(2)}) copy-start(bf16[16,96,512]{2,1,0:T(8,128)(2,1)} %get-tuple-element.7) | copy-start | bytes 4718596
  49.0 0.7 copy-start.2
  49.7 0.7 copy-start.3
  50.4 0.7 copy-start.4
  51.1 0.7 copy-start.5
  51.8 0.7 copy-start.6
  52.4 0.7 copy-start.7

commit v3 on v2

--- a/solution.py
+++ b/solution.py
@@ -37,41 +37,67 @@
     pl.semaphore_wait(barrier, len(targets))
 
 
-def gather_kernel(raw, out, rim, zsend, zrecv, ysend, yrecv, tsend, trecv, lsem, rsend, rrecv):
+def gather_kernel(raw, out, rim, zsend, zrecv, ysend, yrecv, lsem, rootsend, rsend, rrecv):
     seq = lax.axis_index("seq")
     head = lax.axis_index("head")
     z = head // 2
     yl = head % 2
-    right = ((z + 1) % NZ) * 2 + yl
-    left = ((z + NZ - 1) % NZ) * 2 + yl
     mate = z * 2 + 1 - yl
     after = (seq + 1) % NSEQ
     before = (seq + NSEQ - 1) % NSEQ
-    greet([{"head": right}, {"head": left}, {"head": mate}, {"seq": after}, {"seq": before}])
-    sides = (right, left)
-
-    def window(turn):
-        return pl.multiple_of(32 * yl + 16 * (turn + yl * (3 - 2 * turn)), 16)
-
-    def span(start, size):
-        return pl.ds(pl.multiple_of(start, 16), size)
-
-    def ring(side, step, turn, slot, src):
+    is_root = head == 2 * NZ - 1
+    is_relay = (yl == 1) & (z % 4 == 3)
+    relay = ((4 * ((z + 2) // 4) + NZ - 1) % NZ) * 2 + 1
+
+    def along(side, by):
+        return ((z + (by if side == 0 else NZ - by)) % NZ) * 2 + yl
+
+    barrier = pltpu.get_barrier_semaphore()
+
+    def greet_one(where):
+        pl.semaphore_signal(
+            barrier, inc=1, device_id=where, device_id_type=pl.DeviceIdType.MESH
+        )
+
+    for side in range(2):
+        for by in (1, 2):
+            greet_one({"head": along(side, by)})
+    greet_one({"head": mate})
+
+    @pl.when(is_relay)
+    def _():
+        greet_one({"seq": before, "head": 2 * NZ - 1})
+
+    @pl.when(jnp.logical_not(is_relay))
+    def _():
+        greet_one({"head": relay})
+
+    pl.semaphore_wait(
+        barrier, 5 + 4 * is_root.astype(jnp.int32) + 7 * is_relay.astype(jnp.int32)
+    )
+
+    own_rows = pl.ds(pl.multiple_of(48 * yl, 16), 48)
+    mate_rows = pl.ds(pl.multiple_of(48 - 48 * yl, 16), 48)
+
+    def slot_of(side, far):
+        return (z + (NZ - far if side == 0 else far)) % NZ
+
+    def hop(side, far, slot, first=False):
+        start, size = (48 * yl, 48) if far < 8 else (48 * yl + 32 * side, 32 - 16 * side)
+        rows = pl.ds(pl.multiple_of(start, 16), size)
+        there = out.at[slot, rows]
         return remote(
-            src,
-            out.at[slot, span(window(turn), 16)],
-            zsend.at[side, step, turn],
-            zrecv.at[side, step, turn],
-            head=sides[side],
-        )
-
-    def across(index, slot, src):
+            raw if first else there,
+            there,
+            zsend.at[side, far],
+            zrecv.at[side, far],
+            head=along(side, 1 if far == 1 else 2),
+        )
+
+    def across(index, slot, src=None):
+        there = out.at[slot, own_rows]
         return remote(
-            src,
-            out.at[slot, span(64 * yl, 32)],
-            ysend.at[index],
-            yrecv.at[index],
-            head=mate,
+            there if src is None else src, there, ysend.at[index], yrecv.at[index], head=mate
         )
 
     sent = []
@@ -80,57 +106,76 @@
         copy.start()
         sent.append(copy)
 
-    middle = remote(
-        raw.at[span(32 - 32 * yl, 16)],
-        out.at[z, span(32 + 16 * yl, 16)],
-        tsend,
-        trecv,
-        head=mate,
-    )
-    go(middle)
-    for turn in range(3):
+    for side in range(2):
+        go(hop(side, 2, z, True))
+        go(hop(side, 1, z, True))
+    go(across(0, z, raw))
+
+    def from_root(group):
+        return remote(
+            raw.at[pl.ds(32, 16)],
+            rim,
+            rootsend.at[group],
+            rrecv,
+            seq=after,
+            head=(4 * group + 3) * 2 + 1,
+        )
+
+    def from_relay(index):
+        by, column = ((0, 0), (1, 0), (1, 1), (2, 0), (2, 1), (NZ - 1, 0), (NZ - 1, 1))[index]
+        return remote(rim, rim, rsend.at[index], rrecv, head=((z + by) % NZ) * 2 + column)
+
+    @pl.when(is_root)
+    def _():
+        for group in range(4):
+            from_root(group).start()
+
+    own = pltpu.make_async_copy(raw, out.at[z, own_rows], lsem)
+    own.start()
+    for far in range(1, 9):
         for side in range(2):
-            go(ring(side, 0, turn, z, raw.at[span(window(turn) - 48 * yl, 16)]))
-    go(across(0, z, raw.at[span(16 * yl, 32)]))
-    own = pltpu.make_async_copy(raw, out.at[z, span(48 * yl, 48)], lsem)
-    own.start()
-    remote(
-        raw.at[span(32 - 32 * yl, 16)],
-        out.at[z, span(48 - 16 * yl, 16)],
-        tsend,
-        trecv,
-        head=mate,
-    ).wait_recv()
-    for side in range(2):
-        go(ring(side, 0, 3, z, out.at[z, span(window(3), 16)]))
-    for step in range(1, 9):
-        slots = ((z + NZ - step) % NZ, (z + step) % NZ)
-        for turn in range(4):
-            for side in range(2):
-                if step == 8 and side != turn // 2:
-                    continue
-                slot = slots[side]
-                piece = out.at[slot, span(window(turn), 16)]
-                ring(side, step - 1, turn, slot, piece).wait_recv()
-                if step < 7 or (step == 7 and side == turn // 2):
-                    go(ring(side, step, turn, slot, piece))
-                if turn == 1:
-                    index = step + 8 * side
-                    go(across(index, slot, out.at[slot, span(64 * yl, 32)]))
+            slot = slot_of(side, far)
+            hop(side, far, slot).wait_recv()
+            if far + 2 <= 8:
+                go(hop(side, far + 2, slot))
+            if far < 8:
+                go(across(far + 8 * side, slot))
+        if far == 6:
+
+            @pl.when(is_relay)
+            def _():
+                from_root(0).wait_recv()
+                for index in range(7):
+                    from_relay(index).start()
+
+    go(across(8, slot_of(0, 8)))
     for index in range(16):
-        slot = (z + NZ - index) % NZ if index <= 8 else (z + index - 8) % NZ
-        landed = out.at[slot, span(64 * (1 - yl), 32)]
+        slot = slot_of(0, index) if index <= 8 else slot_of(1, index - 8)
+        landed = out.at[slot, mate_rows]
         remote(landed, landed, ysend.at[index], yrecv.at[index], head=mate).wait_recv()
     own.wait()
-    edge = remote(out.at[NZ - 1, pl.ds(80, 16)], rim, rsend, rrecv, seq=after)
-    edge.start()
+
+    @pl.when(jnp.logical_not(is_relay))
+    def _():
+        from_root(0).wait_recv()
+
+    @pl.when(is_relay)
+    def _():
+        for index in range(7):
+            from_relay(index).wait_send()
+
+    @pl.when(is_root)
+    def _():
+        for group in range(4):
+            from_root(group).wait_send()
+
     for copy in sent:
         copy.wait_send()
-    edge.wait()
 
 
 def gather(raw):
     rows, width = raw.shape
+    dma = pltpu.SemaphoreType.DMA
     return pl.pallas_call(
         gather_kernel,
         out_shape=(
@@ -140,17 +185,18 @@
         in_specs=[VMEM_SPEC],
         out_specs=(VMEM_SPEC, VMEM_SPEC),
         scratch_shapes=[
-            pltpu.SemaphoreType.DMA((2, 8, 4)),
-            pltpu.SemaphoreType.DMA((2, 8, 4)),
-            pltpu.SemaphoreType.DMA((16,)),
-            pltpu.SemaphoreType.DMA((16,)),
-            pltpu.SemaphoreType.DMA,
-            pltpu.SemaphoreType.DMA,
-            pltpu.SemaphoreType.DMA,
-            pltpu.SemaphoreType.DMA,
-            pltpu.SemaphoreType.DMA,
+            dma((2, 9)),
+            dma((2, 9)),
+            dma((16,)),
+            dma((16,)),
+            dma,
+            dma((4,)),
+            dma((7,)),
+            dma,
         ],
-        compiler_params=pltpu.CompilerParams(collective_id=0, has_side_effects=True),
+        compiler_params=pltpu.CompilerParams(
+            collective_id=0, has_side_effects=True, vmem_limit_bytes=8 * 1024 * 1024
+        ),
         name="gather_bc",
     )(raw)
 

time: 93.7 us -> 85.8 us (0.916)
  Pallas kernels: 84.4 us -> 78 us
  local copies, waits for them, and re-layouts: 8.78 us -> 7.46 us
    pallas_call x1, Pallas kernels: 45.4 us -> 35.2 us  [gather(): pl.pallas_call(gather_kernel, out_shape=(jax.ShapeDtypeStruct((NZ, 2 * ro...]
    pallas_call x1, Pallas kernels: 39 us -> 42.8 us  [mixer(): pl.pallas_call(mixer_kernel, out_shape=jax.ShapeDtypeStruct((length, widt...]
    unnamed x17 -> x15, local copies, waits for them, and re-layouts: 8.04 us -> 6.71 us
where the time goes in v3:
time: 85.8 us; the launch traced here: 85.4 us
  Pallas kernels  78 us (91%)
  local copies, waits for them, and re-layouts  7.46 us (9%)
    pallas_call x1, Pallas kernels, mixer(): pl.pallas_call(mixer_kernel, out_shape=jax.ShapeDtypeStruct((length, widt...  42.8 us
    pallas_call x1, Pallas kernels, gather(): pl.pallas_call(gather_kernel, out_shape=(jax.ShapeDtypeStruct((NZ, 2 * ro...  35.2 us
    unnamed x15, local copies, waits for them, and re-layouts  6.71 us

profile of v3, /device:TPU:8, one launch (start us, length us, event | category | flops | bytes accessed | tf_op | source)
XLA Modules:
  0.0 85.4 jit_solution(6911778937102176080)
XLA Ops:
  0.0 0.7 pad.4
  0.7 0.0 copy-start.1
  0.7 0.8 copy-done.1
  1.5 35.2 %gather_bc.1 = (bf16[16,96,512]{2,1,0:T(8,128)(2,1)S(1)}, bf16[16,512]{1,0:T(8,128)(2,1)S(1)}) custom-call(bf16[48,512]{1,0:T(8,128)(2,1)S(1)} %copy-done.1), custom_call_target="tpu_custom_call" | custom-call | tf_op jit(solution)/shard_map/gather_bc/pallas_call | solution.py:179
  36.7 0.0 copy-start
  36.8 1.4 %copy-done = bf16[1536,512]{1,0:T(8,128)(2,1)S(1)} copy-done((bf16[1536,512]{1,0:T(8,128)(2,1)S(1)}, bf16[1536,512]{1,0:T(8,128)(2,1)}, u32[]{:S(2)}) %copy-start) | copy-done | bytes 1572888
  38.2 0.0 copy-start.2
  38.2 0.7 copy-done.2
  38.9 0.0 copy-start.3
  38.9 0.7 copy-done.3
  39.5 0.0 copy-start.4
  39.5 0.7 copy-done.4
  40.2 0.0 copy-start.5
  40.2 0.7 copy-done.5
  40.9 0.0 copy-start.6
  40.9 0.7 copy-done.6
  41.5 42.8 %mixer.1 = bf16[1536,512]{1,0:T(8,128)(2,1)S(1)} custom-call(f32[4]{0:T(128)S(1)} %copy-done.5, f32[4]{0:T(128)S(1)} %copy-done.6, bf16[1536,512]{1,0:T(8,128)(2,1)S(1)} %bitcast.7, bf16[16,512]{1,0:T(8,128)(2,1)S(1)} %get-tuple-element.8.rim, f32[4,512]{1,0:T(4,128)S(1)} %copy-done.2, f32[1,512]{1,0:T(1,128)S(1)} %bitcast.9, f32[6,8,256]{2,1,0:T(8,128)S(1)} %bitcast.8, ...), custom_call_target="tpu_custom_call" | custom-call | tf_op jit(solution)/shard_map/mixer/pallas_call | solution.py:444
  84.3 1.1 %copy.11 = bf16[1536,512]{1,0:T(8,128)(2,1)} copy(bf16[1536,512]{1,0:T(8,128)(2,1)S(1)} %mixer.1) | data formatting | bytes 3145728
Async XLA Ops:
  0.7 0.8 copy-start.1
  36.7 1.4 %copy-start = (bf16[1536,512]{1,0:T(8,128)(2,1)S(1)}, bf16[1536,512]{1,0:T(8,128)(2,1)}, u32[]{:S(2)}) copy-start(bf16[1536,512]{1,0:T(8,128)(2,1)} %x_far.1) | copy-start | bytes 4718596
  38.2 0.7 copy-start.2
  38.9 0.7 copy-start.3
  39.5 0.7 copy-start.4
  40.2 0.7 copy-start.5
  40.9 0.7 copy-start.6

commit v4 on v3

--- a/solution.py
+++ b/solution.py
@@ -12,7 +12,6 @@
 NSEQ = 16
 NZ = 16
 VMEM_SPEC = pl.BlockSpec(memory_space=pltpu.VMEM)
-SMEM_SPEC = pl.BlockSpec(memory_space=pltpu.SMEM)
 F32 = jnp.float32
 BF16 = jnp.bfloat16
 
@@ -222,14 +221,10 @@
 
 
 def mixer_kernel(
-    a_log,
-    d_skip,
     raw,
     rim,
-    conv_weight,
-    conv_bias,
+    small,
     dt,
-    gain,
     x_far,
     z_far,
     out,
@@ -289,11 +284,7 @@
     def rows_of(block):
         return pl.ds(pl.multiple_of(block * BLOCK, BLOCK), BLOCK)
 
-    sub = lax.broadcasted_iota(jnp.int32, (8, BLOCK), 0)
-    rate = jnp.full((8, BLOCK), a_log[0], F32)
-    for h in range(1, 4):
-        rate = jnp.where(sub == h, a_log[h], rate)
-    rate = -jnp.exp(rate)
+    rate = small[8:16, 0:BLOCK]
     row = lax.broadcasted_iota(jnp.int32, (BLOCK, BLOCK), 0)
     column = lax.broadcasted_iota(jnp.int32, (BLOCK, BLOCK), 1)
     upper = jnp.where(row <= column, 1.0, 0.0).astype(BF16)
@@ -306,9 +297,9 @@
     def first_pass(block, _):
         rows = rows_of(block)
         padded[8 : 8 + BLOCK, :] = raw[rows, :].astype(F32)
-        summed = jnp.broadcast_to(conv_bias[...], (BLOCK, 2 * STATE))
+        summed = jnp.broadcast_to(small[4:5, :], (BLOCK, 2 * STATE))
         for tap in range(4):
-            summed = summed + conv_weight[tap : tap + 1, :] * padded[5 + tap : 5 + tap + BLOCK, :]
+            summed = summed + small[tap : tap + 1, :] * padded[5 + tap : 5 + tap + BLOCK, :]
         acted = jax.nn.silu(summed).astype(BF16)
         act[rows, :] = acted
         padded[0:8, :] = padded[BLOCK : BLOCK + 8, :]
@@ -363,7 +354,7 @@
             x_head = x_ref[rows, lanes]
             mixed[rows, lanes] = dot(
                 (gram * decay).astype(BF16), x_head, 1, 0
-            ) + d_skip[h] * x_head.astype(F32)
+            ) + small[6:7, lanes] * x_head.astype(F32)
         return 0
 
     lax.fori_loop(0, blocks // 2, inner_pass, 0)
@@ -428,7 +419,7 @@
     def norm_pass(part, _):
         rows = pl.ds(pl.multiple_of(part * 128, 128), 128)
         inverse = jnp.transpose(jnp.broadcast_to(pair[pl.ds(part, 1), :], (8, 128)))[:, 0:1]
-        out[rows, :] = (mixed[rows, :] * inverse * gain[...]).astype(BF16)
+        out[rows, :] = (mixed[rows, :] * inverse * small[5:6, :]).astype(BF16)
         return 0
 
     lax.fori_loop(0, 2 * blocks, norm_pass, 0)
@@ -436,7 +427,7 @@
         copy.wait_send()
 
 
-def mixer(raw, rim, conv_weight, conv_bias, dt, a_log, d_skip, gain, x, z_gate):
+def mixer(raw, rim, small, dt, x, z_gate):
     length, width = x.shape
     blocks = length // BLOCK
     far = pl.BlockSpec(memory_space=pl.ANY)
@@ -444,7 +435,7 @@
     return pl.pallas_call(
         mixer_kernel,
         out_shape=jax.ShapeDtypeStruct((length, width), BF16),
-        in_specs=[SMEM_SPEC, SMEM_SPEC] + [VMEM_SPEC] * 6 + [far, far],
+        in_specs=[VMEM_SPEC] * 4 + [far, far],
         out_specs=VMEM_SPEC,
         scratch_shapes=[
             pltpu.VMEM((length, width), BF16),
@@ -475,27 +466,28 @@
             collective_id=1, has_side_effects=True, vmem_limit_bytes=48 * 1024 * 1024
         ),
         name="mixer",
-    )(a_log, d_skip, raw, rim, conv_weight, conv_bias, dt, gain, x, z_gate)
+    )(raw, rim, small, dt, x, z_gate)
 
 
 def on_device(x_inner, z_gate, bc_raw, conv_weight, conv_bias, dt_raw, a_log, d_skip, norm_gain):
     length = x_inner.shape[0]
     dt = jnp.pad(dt_raw.T, ((0, 4), (0, 0)))
     dt = jnp.transpose(dt.reshape(8, length // BLOCK, BLOCK), (1, 0, 2))
+    width = 2 * STATE
+    small = jnp.concatenate(
+        [
+            conv_weight,
+            conv_bias[None, :],
+            norm_gain[None, :],
+            jnp.repeat(d_skip, HEAD_DIM)[None, :],
+            jnp.zeros((1, width), F32),
+            jnp.broadcast_to(jnp.pad(-jnp.exp(a_log), (0, 4))[:, None], (8, width)),
+        ],
+        axis=0,
+    )
     gathered, rim = gather(bc_raw)
     raw = gathered.reshape(length, 2 * STATE)
-    return mixer(
-        raw,
-        rim,
-        conv_weight,
-        conv_bias[None, :],
-        dt,
-        a_log,
-        d_skip,
-        norm_gain[None, :],
-        x_inner,
-        z_gate,
-    )
+    return mixer(raw, rim, small, dt, x_inner, z_gate)
 
 
 def solution(mesh):

time: 85.8 us -> 84.1 us (0.980)
  local copies, waits for them, and re-layouts: 7.46 us -> 5.64 us
    unnamed x15 -> x5, local copies, waits for them, and re-layouts: 6.71 us -> 3.35 us
where the time goes in v4:
time: 84.1 us; the launch traced here: 83.7 us
  Pallas kernels  77.4 us (92%)
  local copies, waits for them, and re-layouts  5.64 us (7%)
    pallas_call x1, Pallas kernels, mixer(): pl.pallas_call(mixer_kernel, out_shape=jax.ShapeDtypeStruct((length, widt...  42.2 us
    pallas_call x1, Pallas kernels, gather(): pl.pallas_call(gather_kernel, out_shape=(jax.ShapeDtypeStruct((NZ, 2 * ro...  35.2 us
    unnamed x5, local copies, waits for them, and re-layouts  3.35 us

profile of v4, /device:TPU:8, one launch (start us, length us, event | category | flops | bytes accessed | tf_op | source)
XLA Modules:
  0.0 83.7 jit_solution(15301142419545605711)
XLA Ops:
  0.0 0.7 exponential_negate_fusion
  0.7 0.7 broadcast_in_dim.20
  1.4 0.1 broadcast_in_dim.22
  1.5 0.7 concatenate.3.small
  2.2 0.7 pad.9
  3.0 0.0 copy-start.1
  3.0 0.8 copy-done.1
  3.8 35.2 %gather_bc.1 = (bf16[16,96,512]{2,1,0:T(8,128)(2,1)S(1)}, bf16[16,512]{1,0:T(8,128)(2,1)S(1)}) custom-call(bf16[48,512]{1,0:T(8,128)(2,1)S(1)} %copy-done.1), custom_call_target="tpu_custom_call" | custom-call | tf_op jit(solution)/shard_map/gather_bc/pallas_call | solution.py:178
  39.0 0.0 copy-start
  39.0 1.4 %copy-done = bf16[1536,512]{1,0:T(8,128)(2,1)S(1)} copy-done((bf16[1536,512]{1,0:T(8,128)(2,1)S(1)}, bf16[1536,512]{1,0:T(8,128)(2,1)}, u32[]{:S(2)}) %copy-start) | copy-done | bytes 1572888
  40.4 42.2 %mixer.1 = bf16[1536,512]{1,0:T(8,128)(2,1)S(1)} custom-call(bf16[1536,512]{1,0:T(8,128)(2,1)S(1)} %bitcast.8, bf16[16,512]{1,0:T(8,128)(2,1)S(1)} %get-tuple-element.8.rim, f32[16,512]{1,0:T(8,128)S(1)} %concatenate.3.small, f32[6,8,256]{2,1,0:T(8,128)S(1)} %bitcast.9, bf16[1536,512]{1,0:T(8,128)(2,1)S(1)} %copy-done, bf16[1536,512]{1,0:T(8,128)(2,1)} %z_far.1), custom_call_target="tpu_custom_call" | custom-call | tf_op jit(solution)/shard_map/mixer/pallas_call | solution.py:435
  82.6 1.1 %copy.11 = bf16[1536,512]{1,0:T(8,128)(2,1)} copy(bf16[1536,512]{1,0:T(8,128)(2,1)S(1)} %mixer.1) | data formatting | bytes 3145728
  (2 shorter events, 0.0 us)
Async XLA Ops:
  3.0 0.8 copy-start.1
  39.0 1.4 %copy-start = (bf16[1536,512]{1,0:T(8,128)(2,1)S(1)}, bf16[1536,512]{1,0:T(8,128)(2,1)}, u32[]{:S(2)}) copy-start(bf16[1536,512]{1,0:T(8,128)(2,1)} %x_far.1) | copy-start | bytes 4718596
